TPU v7x, 256 devices: a whole 4x4x8 slice. The times are simulated.
256 devices in a mesh: row: 16 (over x_lo, z), col: 16 (over x_hi, y, core).
Axes of the slice: x: 4 (x_hi: 2, x_lo: 2; x = x_hi * 2 + x_lo), y: 4, z: 8, core: 2. Of those that a mesh axis runs over, the one named last changes fastest.
Arguments:
- tensor: bfloat16 [4096, 2048, 128], P('row', 'col'), may hold values from -96 to 96
- factor_a: float32 [4096, 128], P(('row', 'col')), may hold values from -4.5 to 4.5
- factor_b: float32 [2048, 128], P(('col', 'row')), may hold values from -4.5 to 4.5
- factor_c: float32 [128, 128], replicated, may hold values from -4.5 to 4.5
Outputs:
- new_a: float32 [4096, 128], P(('row', 'col'))
- new_b: float32 [2048, 128], P(('col', 'row'))
- new_c: float32 [128, 128], replicated
All inputs are finite; a program needn't handle non-finite values.
Results may differ from a plain program's by a relative error of at most 0.01.
Values may be sent and summed in bfloat16 or wider, within the bound.
A program may use at most 128 MiB of HBM per device.

v0:
```python
import jax
import jax.numpy as jnp
from jax import lax
from jax.sharding import PartitionSpec as P

STEPS = 2
damping = 0.9
scaling = 0.25
epsilon = 1e-06


def column_squares(values16):
    return jnp.sum(jnp.square(values16.astype(jnp.float32)), axis=0)


def local_terms(block, tile_a, tile_b, c16):
    rows_i, rows_j, depth = block.shape
    rank = tile_a.shape[1]
    pairs = (
        tile_a.astype(jnp.float32)[:, None, :] * tile_b.astype(jnp.float32)[None, :, :]
    ).astype(jnp.bfloat16)
    pairs = pairs.reshape(rows_i * rows_j, rank)
    model = jnp.dot(pairs, c16.T, preferred_element_type=jnp.float32)
    resid = (block.reshape(rows_i * rows_j, depth).astype(jnp.float32) - model).astype(jnp.bfloat16)
    along = jnp.dot(resid, c16, preferred_element_type=jnp.float32).reshape(rows_i, rows_j, rank)
    grad_a = jnp.sum(along * tile_b.astype(jnp.float32)[None, :, :], axis=1)
    grad_b = jnp.sum(along * tile_a.astype(jnp.float32)[:, None, :], axis=0)
    grad_c = lax.dot_general(
        resid, pairs, (((0,), (0,)), ((), ())), preferred_element_type=jnp.float32
    )
    return (grad_a, grad_b, grad_c)


def local(tensor, factor_a, factor_b, factor_c):
    own_a, own_b, third = (factor_a, factor_b, factor_c)
    for step in range(STEPS):
        a_mine16 = own_a.astype(jnp.bfloat16)
        b_mine16 = own_b.astype(jnp.bfloat16)
        tile_a = lax.all_gather(a_mine16, "col", axis=0, tiled=True)
        tile_b = lax.all_gather(b_mine16, "row", axis=0, tiled=True)
        norm_a, norm_b = lax.psum(
            (column_squares(a_mine16), column_squares(b_mine16)), ("row", "col")
        )
        c16 = third.astype(jnp.bfloat16)
        norm_c = column_squares(c16)
        step_a = scaling / (norm_b * norm_c + epsilon)
        step_b = scaling / (norm_a * norm_c + epsilon)
        step_c = scaling / (norm_a * norm_b + epsilon)
        grad_a, grad_b, grad_c = local_terms(tensor, tile_a, tile_b, c16)
        grad_a = lax.psum_scatter(
            grad_a.astype(jnp.bfloat16), "col", scatter_dimension=0, tiled=True
        ).astype(jnp.float32)
        grad_b = lax.psum_scatter(
            grad_b.astype(jnp.bfloat16), "row", scatter_dimension=0, tiled=True
        ).astype(jnp.float32)
        own_a = damping * own_a + step_a * grad_a
        own_b = damping * own_b + step_b * grad_b
        grad_c = lax.psum(grad_c, ("row", "col"))
        third = damping * third + step_c * grad_c
    return (own_a, own_b, third)


def solution(mesh):
    return jax.shard_map(
        local,
        mesh=mesh,
        in_specs=(P("row", "col", None), P(("row", "col"), None), P(("col", "row"), None), P()),
        out_specs=(P(("row", "col"), None), P(("col", "row"), None), P()),
        check_vma=False,
    )
```

profile of v0, /device:TPU:1, one launch (start us, length us, event | category | flops | bytes accessed | tf_op | source)
XLA Modules:
  0.0 663.4 jit_solution(11993279583761159699)
XLA Ops:
  8.0 0.0 copy-start.2
  8.0 0.0 all-reduce.7.cloned.1.call-start
  8.1 0.7 multiply_reduce_fusion.9
  8.8 0.7 multiply_reduce_fusion.7
  9.5 30.3 %all_gather.13 = bf16[128,128]{1,0:T(8,128)(2,1)S(1)} all-gather(bf16[8,128]{1,0:T(8,128)(2,1)S(1)} %get-tuple-element.14), channel_id=1, replica_groups=mesh['row'=16,'col'=16] {'row'}, dimensions={0}, use_global_device_ids=true | all-gather | bytes 34816 | tf_op jit(solution)/shard_map/all_gather | solution.py:40
  39.8 31.7 %all_gather.12 = bf16[256,128]{1,0:T(8,128)(2,1)S(1)} all-gather(bf16[16,128]{1,0:T(8,128)(2,1)S(1)} %get-tuple-element.16), channel_id=1, replica_groups=mesh['row'=16,'col'=16] {'col'}, dimensions={0}, use_global_device_ids=true | all-gather | bytes 69632 | tf_op jit(solution)/shard_map/all_gather | solution.py:39
  71.5 5.6 multiply_convert_fusion.1
  77.1 0.0 copy-done.2
  77.1 8.1 %fusion.1 = bf16[32768,128]{1,0:T(8,128)(2,1)S(1)} fusion(bf16[32768,128]{1,0:T(8,128)(2,1)} %bitcast.21, bf16[32768,128]{1,0:T(8,128)(2,1)} %bitcast.25, f32[128,128]{1,0:T(8,128)S(1)} %copy-done.2), kind=kOutput, calls=%fused_computation.3 | convolution fusion | flops 1086341120 | bytes 25231360 | tf_op jit(solution)/shard_map/dot_general | solution.py:23
  85.2 0.0 copy-start
  85.2 3.2 copy-done
  88.5 6.4 fusion.11
  94.8 0.0 all-reduce.7.cloned.1.call-update
  94.9 0.0 reduce-scatter.3.cloned.1.call-start
  94.9 12.1 %multiply_reduce_fusion.3 = (bf16[256,128]{1,0:T(8,128)(2,1)}, f32[32768,128]{1,0:T(8,128)}) fusion(f32[128,128]{1,0:T(8,128)S(1)} %convert_element_type.111, bf16[32768,128]{1,0:T(8,128)(2,1)} %copy-done, f32[128,128]{1,0:T(8,128)S(1)} %copy-done.2), kind=kOutput, calls=%fused_computation.8 | convolution fusion | flops 1082114048 | bytes 25362432 | tf_op jit(solution)/shard_map/dot_general | solution.py:25
  107.0 0.0 reduce-scatter.3.cloned.1.call-update
  107.0 0.0 all-reduce.9.cloned.1.call-start
  107.1 0.0 copy-start.7
  107.1 0.0 copy-start.5
  107.1 0.0 copy-start.4
  107.1 7.3 %multiply_reduce_fusion.2 = bf16[128,128]{1,0:T(8,128)(2,1)S(1)} fusion(f32[256,128,128]{2,1,0:T(8,128)} %bitcast.23, f32[256,128]{1,0:T(8,128)S(1)} %convert_element_type.110), kind=kLoop, calls=%fused_computation.7 | loop fusion | flops 8372224 | bytes 16941056 | tf_op jit(solution)/shard_map/reduce_sum | solution.py:27
  114.5 46.3 %all-reduce = bf16[128,128]{1,0:T(8,128)(2,1)S(1)} all-reduce(bf16[128,128]{1,0:T(8,128)(2,1)S(1)} %multiply_reduce_fusion.2), channel_id=3, replica_groups=mesh['row'=16,'col'=16] {'row'}, use_global_device_ids=true, to_apply=%region_8.0.clone | all-reduce | flops 16384 | bytes 65536
  160.8 0.0 copy-done.7
  160.8 0.6 dynamic-slice
  162.0 84.4 %all-reduce.3 = (f32[128]{0:T(128)S(1)}, f32[128]{0:T(128)S(1)}) all-reduce(f32[128]{0:T(128)S(1)} %get-tuple-element.15, f32[128]{0:T(128)S(1)} %get-tuple-element.13), channel_id=1, replica_groups=mesh['row'=16,'col'=16] {'row','col'}, use_global_device_ids=true, to_apply=%region_6.0 | all-reduce | flops 256 | bytes 2048 | tf_op jit(solution)/shard_map/psum | solution.py:41
  246.4 81.7 %all-reduce.7.cloned.1.call-done = f32[128,128]{1,0:T(8,128)} async-done(((f32[128,128]{1,0:T(8,128)}), f32[128,128]{1,0:T(8,128)}) %all-reduce.7.cloned.1.call-update) | async-done | bytes 65552 | tf_op jit(solution)/shard_map/psum | solution.py:58
  328.1 0.9 multiply_reduce_fusion.4
  329.0 0.0 copy-done.5
  329.1 24.4 %all_gather.15 = bf16[128,128]{1,0:T(8,128)(2,1)S(1)} all-gather(bf16[8,128]{1,0:T(8,128)(2,1)S(1)} %get-tuple-element.12), channel_id=1, replica_groups=mesh['row'=16,'col'=16] {'row'}, dimensions={0}, use_global_device_ids=true | all-gather | bytes 34816 | tf_op jit(solution)/shard_map/all_gather | solution.py:40
  353.5 0.0 reduce-scatter.3.cloned.1.call-done
  353.5 0.0 copy-done.4
  353.5 0.7 multiply_reduce_fusion.6
  354.2 28.8 %all_gather.14 = bf16[256,128]{1,0:T(8,128)(2,1)S(1)} all-gather(bf16[16,128]{1,0:T(8,128)(2,1)S(1)} %get-tuple-element.10), channel_id=1, replica_groups=mesh['row'=16,'col'=16] {'col'}, dimensions={0}, use_global_device_ids=true | all-gather | bytes 69632 | tf_op jit(solution)/shard_map/all_gather | solution.py:39
  383.0 5.6 multiply_convert_fusion
  388.6 8.1 %fusion = bf16[32768,128]{1,0:T(8,128)(2,1)S(1)} fusion(bf16[32768,128]{1,0:T(8,128)(2,1)} %bitcast.19, bf16[128,128]{1,0:T(8,128)(2,1)S(1)} %get-tuple-element.8, bf16[32768,128]{1,0:T(8,128)(2,1)} %bitcast.26), kind=kOutput, calls=%fused_computation.1 | convolution fusion | flops 1086324736 | bytes 25198592 | tf_op jit(solution)/shard_map/dot_general | solution.py:23
  396.7 0.0 copy-start.1
  396.8 3.2 copy-done.1
  400.0 6.4 fusion.12
  406.4 12.1 %multiply_reduce_fusion.1 = (bf16[256,128]{1,0:T(8,128)(2,1)}, f32[32768,128]{1,0:T(8,128)}) fusion(f32[128,128]{1,0:T(8,128)S(1)} %convert_element_type.126, bf16[32768,128]{1,0:T(8,128)(2,1)} %copy-done.1, bf16[128,128]{1,0:T(8,128)(2,1)S(1)} %get-tuple-element.8), kind=kOutput, calls=%fused_computation.5 | convolution fusion | flops 1082097664 | bytes 25329664 | tf_op jit(solution)/shard_map/dot_general | solution.py:25
  418.4 0.0 all-reduce.9.cloned.1.call-update
  418.4 0.0 reduce-scatter.5.cloned.1.call-start
  418.5 0.0 copy-start.3
  418.5 0.0 copy-start.6
  418.5 7.3 %multiply_reduce_fusion = bf16[128,128]{1,0:T(8,128)(2,1)S(1)} fusion(f32[256,128,128]{2,1,0:T(8,128)} %bitcast.24, f32[256,128]{1,0:T(8,128)S(1)} %convert_element_type.125), kind=kLoop, calls=%fused_computation.4 | loop fusion | flops 8372224 | bytes 16941056 | tf_op jit(solution)/shard_map/reduce_sum | solution.py:27
  425.8 47.7 %all-reduce.1 = bf16[128,128]{1,0:T(8,128)(2,1)S(1)} all-reduce(bf16[128,128]{1,0:T(8,128)(2,1)S(1)} %multiply_reduce_fusion), channel_id=5, replica_groups=mesh['row'=16,'col'=16] {'row'}, use_global_device_ids=true, to_apply=%region_18.0.clone | all-reduce | flops 16384 | bytes 65536
  473.5 86.2 %all-reduce.2 = (f32[128]{0:T(128)S(1)}, f32[128]{0:T(128)S(1)}) all-reduce(f32[128]{0:T(128)S(1)} %get-tuple-element.11, f32[128]{0:T(128)S(1)} %get-tuple-element.9), channel_id=1, replica_groups=mesh['row'=16,'col'=16] {'row','col'}, use_global_device_ids=true, to_apply=%region_10.0 | all-reduce | flops 256 | bytes 2048 | tf_op jit(solution)/shard_map/psum | solution.py:41
  559.7 0.6 multiply_add_fusion.4
  560.3 0.0 reduce-scatter.5.cloned.1.call-update
  560.3 92.8 %all-reduce.9.cloned.1.call-done = f32[128,128]{1,0:T(8,128)} async-done(((f32[128,128]{1,0:T(8,128)}), f32[128,128]{1,0:T(8,128)}) %all-reduce.9.cloned.1.call-update) | async-done | bytes 65552 | tf_op jit(solution)/shard_map/psum | solution.py:58
  653.2 0.0 copy-done.3
  653.2 1.5 multiply_add_fusion
  654.6 0.0 reduce-scatter.5.cloned.1.call-done
  654.6 0.0 copy-done.6
  654.6 1.3 multiply_add_fusion.2
  (8 shorter events, 0.1 us)
Async XLA Ops:
  8.0 69.1 %copy-start.2 = (f32[128,128]{1,0:T(8,128)S(1)}, f32[128,128]{1,0:T(8,128)}, u32[]{:S(2)}) copy-start(f32[128,128]{1,0:T(8,128)} %param.7) | copy-start | bytes 196612
  8.0 320.1 %all-reduce.7.cloned.1.call-start = ((), (), s32[]{:S(2)}) async-start(), calls=%async_computation.3 | async-start | bytes 131072 | tf_op jit(solution)/shard_map/psum | solution.py:58
  85.2 3.2 copy-start
  94.9 258.6 %reduce-scatter.3.cloned.1.call-start = ((), (), s32[]{:S(2)}) async-start(), calls=%async_computation.2 | async-start | bytes 69632 | tf_op jit(solution)/shard_map/reduce_scatter | solution.py:50
  107.0 546.1 %all-reduce.9.cloned.1.call-start = ((), (), s32[]{:S(2)}) async-start(), calls=%async_computation.5 | async-start | bytes 131072 | tf_op jit(solution)/shard_map/psum | solution.py:58
  107.1 53.7 %copy-start.7 = (u32[256]{0:T(256)S(1)}, u32[256]{0:T(256)}, u32[]{:S(2)}) copy-start(u32[256]{0:T(256)} %constant.14) | copy-start | bytes 3076
  107.1 221.9 %copy-start.5 = (f32[8,128]{1,0:T(8,128)S(1)}, f32[8,128]{1,0:T(8,128)}, u32[]{:S(2)}) copy-start(f32[8,128]{1,0:T(8,128)} %param.6) | copy-start | bytes 12292
  107.1 246.4 %copy-start.4 = (f32[16,128]{1,0:T(8,128)S(1)}, f32[16,128]{1,0:T(8,128)}, u32[]{:S(2)}) copy-start(f32[16,128]{1,0:T(8,128)} %param.5) | copy-start | bytes 24580
  396.7 3.2 copy-start.1
  418.4 236.2 %reduce-scatter.5.cloned.1.call-start = ((), (), s32[]{:S(2)}) async-start(), calls=%async_computation.4 | async-start | bytes 69632 | tf_op jit(solution)/shard_map/reduce_scatter | solution.py:50
  418.5 234.7 %copy-start.3 = (f32[128,128]{1,0:T(8,128)S(1)}, f32[128,128]{1,0:T(8,128)}, u32[]{:S(2)}) copy-start(f32[128,128]{1,0:T(8,128)} %all-reduce.7.cloned.1.call-done) | copy-start | bytes 196612
  418.5 236.1 %copy-start.6 = (bf16[16,128]{1,0:T(8,128)(2,1)S(1)}, bf16[16,128]{1,0:T(8,128)(2,1)}, u32[]{:S(2)}) copy-start(bf16[16,128]{1,0:T(8,128)(2,1)} %reduce-scatter.3.cloned.1.call-done) | copy-start | bytes 12292
Sparse Core Ops, SparseCore 0:
  95.0 233.1 all-reduce.6
  418.6 234.5 all-reduce.8
Sparse Core Ops, SparseCore 1:
  107.1 58.3 reduce-scatter.2
  560.4 60.9 reduce-scatter.4
where the time goes:
time: 664 us; the launch traced here: 663 us
  blocking collectives  380 us (57%)
  waiting for transfers between devices  175 us (26%)
  matrix products  53.2 us (8%)
  other arithmetic  32.4 us (5%)
  between operations  16.3 us (2%)
  local copies, waits for them, and re-layouts  7.04 us (1%)
    psum x2, waiting for transfers between devices, local(): grad_c = lax.psum(grad_c, ('row', 'col'))  175 us
    psum x2, blocking collectives, local(): lax.psum((column_squares(a_mine16), column_squares(b_mine16)), ('row', 'c...  171 us
    unnamed x2, blocking collectives  94 us
    all_gather x2, blocking collectives, local(): tile_a = lax.all_gather(a_mine16, 'col', axis=0, tiled=True)  60.5 us
    all_gather x2, blocking collectives, local(): tile_b = lax.all_gather(b_mine16, 'row', axis=0, tiled=True)  54.7 us
    dot_general x2, matrix products, local_terms(): jnp.dot(resid, c16, preferred_element_type=jnp.float32)  24.1 us
    dot_general x2, matrix products, local_terms(): model = jnp.dot(pairs, c16.T, preferred_element_type=jnp.float32)  16.2 us
    reduce_sum x2, other arithmetic, local_terms(): grad_b = jnp.sum(along * tile_a.astype(jnp.float32)[:, None, :], axis=0)  14.7 us
  transfers between devices with their start and end apart: 4, of which 2 were waited for; matrix products, arithmetic and copies ran while one was open for 5% of the time, Pallas kernels for 0%

commit v1 on v0

--- a/solution.py
+++ b/solution.py
@@ -55,7 +55,8 @@
         ).astype(jnp.float32)
         own_a = damping * own_a + step_a * grad_a
         own_b = damping * own_b + step_b * grad_b
-        grad_c = lax.psum(grad_c, ("row", "col"))
+        for mesh_axis in ("row", "col"):
+            grad_c = lax.psum(grad_c, mesh_axis)
         third = damping * third + step_c * grad_c
     return (own_a, own_b, third)
 

time: 664 us -> 836 us (1.26)
  waiting for transfers between devices: 175 us -> 344 us
    reduce_scatter x2, waiting for transfers between devices: 0.02 us -> 97.6 us  [local(): lax.psum_scatter(grad_a.astype(jnp.bfloat16), 'col', scatter_dimension=0,...]
    psum x2 -> x4, waiting for transfers between devices: 175 us -> 246 us  [local(): grad_c = lax.psum(grad_c, mesh_axis)]
  transfers between devices with their start and end apart: 4 -> 6, of which waited for: 2 -> 4; matrix products, arithmetic and copies ran while one was open for 5% -> 4% of each run, Pallas kernels for 0% -> 0%
where the time goes in v1:
time: 836 us; the launch traced here: 834 us
  blocking collectives  382 us (46%)
  waiting for transfers between devices  344 us (41%)
  matrix products  53.1 us (6%)
  other arithmetic  32.3 us (4%)
  between operations  14.9 us (2%)
    psum x4, waiting for transfers between devices, local(): grad_c = lax.psum(grad_c, mesh_axis)  246 us
    psum x2, blocking collectives, local(): lax.psum((column_squares(a_mine16), column_squares(b_mine16)), ('row', 'c...  174 us
    reduce_scatter x2, waiting for transfers between devices, local(): lax.psum_scatter(grad_a.astype(jnp.bfloat16), 'col', scatter_dimension=0,...  97.6 us
    unnamed x2, blocking collectives  97.2 us
    all_gather x2, blocking collectives, local(): tile_a = lax.all_gather(a_mine16, 'col', axis=0, tiled=True)  56.3 us
    all_gather x2, blocking collectives, local(): tile_b = lax.all_gather(b_mine16, 'row', axis=0, tiled=True)  55.2 us
    dot_general x2, matrix products, local_terms(): jnp.dot(resid, c16, preferred_element_type=jnp.float32)  24.1 us
  transfers between devices with their start and end apart: 6, of which 4 were waited for; matrix products, arithmetic and copies ran while one was open for 4% of the time, Pallas kernels for 0%

profile of v1, /device:TPU:1, one launch (start us, length us, event | category | flops | bytes accessed | tf_op | source)
XLA Modules:
  0.0 833.8 jit_solution(12217615155700573292)
XLA Ops:
  7.2 0.0 copy-start.2
  7.2 0.0 all-reduce.9.cloned.1.call-start
  7.2 0.7 multiply_reduce_fusion.9
  7.9 0.7 multiply_reduce_fusion.7
  8.6 30.3 %all_gather.13 = bf16[128,128]{1,0:T(8,128)(2,1)S(1)} all-gather(bf16[8,128]{1,0:T(8,128)(2,1)S(1)} %get-tuple-element.14), channel_id=1, replica_groups=mesh['row'=16,'col'=16] {'row'}, dimensions={0}, use_global_device_ids=true | all-gather | bytes 34816 | tf_op jit(solution)/shard_map/all_gather | solution.py:40
  38.9 31.7 %all_gather.12 = bf16[256,128]{1,0:T(8,128)(2,1)S(1)} all-gather(bf16[16,128]{1,0:T(8,128)(2,1)S(1)} %get-tuple-element.16), channel_id=1, replica_groups=mesh['row'=16,'col'=16] {'col'}, dimensions={0}, use_global_device_ids=true | all-gather | bytes 69632 | tf_op jit(solution)/shard_map/all_gather | solution.py:39
  70.7 5.6 multiply_convert_fusion.1
  76.3 0.0 copy-done.2
  76.3 8.1 fusion.1
  84.4 0.0 copy-start
  84.4 3.2 copy-done
  87.6 6.4 fusion.11
  94.0 0.0 all-reduce.9.cloned.1.call-update
  94.0 0.0 all-reduce.11.cloned.1.call-start
  94.1 110.6 %all-reduce.9.cloned.1.call-done = f32[128,128]{1,0:T(8,128)} async-done(((f32[128,128]{1,0:T(8,128)}), f32[128,128]{1,0:T(8,128)}) %all-reduce.9.cloned.1.call-update) | async-done | bytes 65552 | tf_op jit(solution)/shard_map/psum | solution.py:59
  204.7 0.0 all-reduce.11.cloned.1.call-update
  204.7 0.0 reduce-scatter.3.cloned.1.call-start
  204.7 12.1 %multiply_reduce_fusion.3 = (bf16[256,128]{1,0:T(8,128)(2,1)}, f32[32768,128]{1,0:T(8,128)}) fusion(f32[128,128]{1,0:T(8,128)S(1)} %convert_element_type.111, bf16[32768,128]{1,0:T(8,128)(2,1)} %copy-done, f32[128,128]{1,0:T(8,128)S(1)} %copy-done.2), kind=kOutput, calls=%fused_computation.8 | convolution fusion | flops 1082114048 | bytes 25362432 | tf_op jit(solution)/shard_map/dot_general | solution.py:25
  216.8 0.0 reduce-scatter.3.cloned.1.call-update
  216.8 0.0 all-reduce.13.cloned.1.call-start
  216.9 0.0 copy-start.7
  216.9 0.0 copy-start.5
  216.9 0.0 copy-start.4
  216.9 7.3 multiply_reduce_fusion.2
  224.2 48.5 %all-reduce = bf16[128,128]{1,0:T(8,128)(2,1)S(1)} all-reduce(bf16[128,128]{1,0:T(8,128)(2,1)S(1)} %multiply_reduce_fusion.2), channel_id=3, replica_groups=mesh['row'=16,'col'=16] {'row'}, use_global_device_ids=true, to_apply=%region_8.0.clone | all-reduce | flops 16384 | bytes 65536
  272.7 0.0 copy-done.7
  272.7 0.6 dynamic-slice
  273.9 97.7 %all-reduce.3 = (f32[128]{0:T(128)S(1)}, f32[128]{0:T(128)S(1)}) all-reduce(f32[128]{0:T(128)S(1)} %get-tuple-element.15, f32[128]{0:T(128)S(1)} %get-tuple-element.13), channel_id=1, replica_groups=mesh['row'=16,'col'=16] {'row','col'}, use_global_device_ids=true, to_apply=%region_6.0 | all-reduce | flops 256 | bytes 2048 | tf_op jit(solution)/shard_map/psum | solution.py:41
  371.7 0.0 all-reduce.11.cloned.1.call-done
  371.7 0.9 multiply_reduce_fusion.4
  372.6 0.0 copy-done.5
  372.6 25.0 %all_gather.15 = bf16[128,128]{1,0:T(8,128)(2,1)S(1)} all-gather(bf16[8,128]{1,0:T(8,128)(2,1)S(1)} %get-tuple-element.12), channel_id=1, replica_groups=mesh['row'=16,'col'=16] {'row'}, dimensions={0}, use_global_device_ids=true | all-gather | bytes 34816 | tf_op jit(solution)/shard_map/all_gather | solution.py:40
  397.6 23.7 %reduce-scatter.3.cloned.1.call-done = bf16[16,128]{1,0:T(8,128)(2,1)} async-done(((bf16[256,128]{1,0:T(8,128)(2,1)}), bf16[16,128]{1,0:T(8,128)(2,1)}) %reduce-scatter.3.cloned.1.call-update) | async-done | bytes 4112 | tf_op jit(solution)/shard_map/reduce_scatter | solution.py:50
  421.3 0.0 copy-done.4
  421.3 0.7 multiply_reduce_fusion.6
  422.0 24.5 %all_gather.14 = bf16[256,128]{1,0:T(8,128)(2,1)S(1)} all-gather(bf16[16,128]{1,0:T(8,128)(2,1)S(1)} %get-tuple-element.10), channel_id=1, replica_groups=mesh['row'=16,'col'=16] {'col'}, dimensions={0}, use_global_device_ids=true | all-gather | bytes 69632 | tf_op jit(solution)/shard_map/all_gather | solution.py:39
  446.6 5.6 multiply_convert_fusion
  452.2 8.1 fusion
  460.3 0.0 copy-start.1
  460.3 3.2 copy-done.1
  463.5 6.4 fusion.12
  469.9 12.1 %multiply_reduce_fusion.1 = (bf16[256,128]{1,0:T(8,128)(2,1)}, f32[32768,128]{1,0:T(8,128)}) fusion(f32[128,128]{1,0:T(8,128)S(1)} %convert_element_type.126, bf16[32768,128]{1,0:T(8,128)(2,1)} %copy-done.1, bf16[128,128]{1,0:T(8,128)(2,1)S(1)} %get-tuple-element.8), kind=kOutput, calls=%fused_computation.5 | convolution fusion | flops 1082097664 | bytes 25329664 | tf_op jit(solution)/shard_map/dot_general | solution.py:25
  482.0 0.0 all-reduce.13.cloned.1.call-update
  482.0 0.0 reduce-scatter.5.cloned.1.call-start
  482.0 0.0 copy-start.6
  482.1 0.0 copy-start.3
  482.1 7.3 multiply_reduce_fusion
  489.4 76.0 %all-reduce.2 = (f32[128]{0:T(128)S(1)}, f32[128]{0:T(128)S(1)}) all-reduce(f32[128]{0:T(128)S(1)} %get-tuple-element.11, f32[128]{0:T(128)S(1)} %get-tuple-element.9), channel_id=1, replica_groups=mesh['row'=16,'col'=16] {'row','col'}, use_global_device_ids=true, to_apply=%region_10.0 | all-reduce | flops 256 | bytes 2048 | tf_op jit(solution)/shard_map/psum | solution.py:41
  565.4 48.8 %all-reduce.1 = bf16[128,128]{1,0:T(8,128)(2,1)S(1)} all-reduce(bf16[128,128]{1,0:T(8,128)(2,1)S(1)} %multiply_reduce_fusion), channel_id=5, replica_groups=mesh['row'=16,'col'=16] {'row'}, use_global_device_ids=true, to_apply=%region_19.0.clone | all-reduce | flops 16384 | bytes 65536
  614.2 0.0 reduce-scatter.5.cloned.1.call-update
  614.2 0.0 all-reduce.15.cloned.1.call-start
  614.3 0.6 multiply_add_fusion.4
  614.9 0.0 all-reduce.13.cloned.1.call-done
  614.9 0.0 all-reduce.15.cloned.1.call-update
  614.9 73.9 %reduce-scatter.5.cloned.1.call-done = bf16[16,128]{1,0:T(8,128)(2,1)} async-done(((bf16[256,128]{1,0:T(8,128)(2,1)}), bf16[16,128]{1,0:T(8,128)(2,1)}) %reduce-scatter.5.cloned.1.call-update) | async-done | bytes 4112 | tf_op jit(solution)/shard_map/reduce_scatter | solution.py:50
  688.8 0.0 copy-done.6
  688.8 1.3 multiply_add_fusion.2
  690.0 135.4 %all-reduce.15.cloned.1.call-done = f32[128,128]{1,0:T(8,128)} async-done(((f32[128,128]{1,0:T(8,128)}), f32[128,128]{1,0:T(8,128)}) %all-reduce.15.cloned.1.call-update) | async-done | bytes 65552 | tf_op jit(solution)/shard_map/psum | solution.py:59
  825.5 0.0 copy-done.3
  825.5 1.5 multiply_add_fusion
  (8 shorter events, 0.1 us)
Async XLA Ops:
  7.2 69.1 %copy-start.2 = (f32[128,128]{1,0:T(8,128)S(1)}, f32[128,128]{1,0:T(8,128)}, u32[]{:S(2)}) copy-start(f32[128,128]{1,0:T(8,128)} %param.7) | copy-start | bytes 196612
  7.2 197.5 %all-reduce.9.cloned.1.call-start = ((), (), s32[]{:S(2)}) async-start(), calls=%async_computation.3 | async-start | bytes 131072 | tf_op jit(solution)/shard_map/psum | solution.py:59
  84.4 3.2 copy-start
  94.0 277.6 %all-reduce.11.cloned.1.call-start = ((), (), s32[]{:S(2)}) async-start(), calls=%async_computation.4 | async-start | bytes 131072 | tf_op jit(solution)/shard_map/psum | solution.py:59
  204.7 216.6 %reduce-scatter.3.cloned.1.call-start = ((), (), s32[]{:S(2)}) async-start(), calls=%async_computation.2 | async-start | bytes 69632 | tf_op jit(solution)/shard_map/reduce_scatter | solution.py:50
  216.8 398.0 %all-reduce.13.cloned.1.call-start = ((), (), s32[]{:S(2)}) async-start(), calls=%async_computation.6 | async-start | bytes 131072 | tf_op jit(solution)/shard_map/psum | solution.py:59
  216.9 55.8 %copy-start.7 = (u32[256]{0:T(256)S(1)}, u32[256]{0:T(256)}, u32[]{:S(2)}) copy-start(u32[256]{0:T(256)} %constant.14) | copy-start | bytes 3076
  216.9 155.7 %copy-start.5 = (f32[8,128]{1,0:T(8,128)S(1)}, f32[8,128]{1,0:T(8,128)}, u32[]{:S(2)}) copy-start(f32[8,128]{1,0:T(8,128)} %param.6) | copy-start | bytes 12292
  216.9 204.4 %copy-start.4 = (f32[16,128]{1,0:T(8,128)S(1)}, f32[16,128]{1,0:T(8,128)}, u32[]{:S(2)}) copy-start(f32[16,128]{1,0:T(8,128)} %param.5) | copy-start | bytes 24580
  460.3 3.2 copy-start.1
  482.0 206.8 %reduce-scatter.5.cloned.1.call-start = ((), (), s32[]{:S(2)}) async-start(), calls=%async_computation.5 | async-start | bytes 69632 | tf_op jit(solution)/shard_map/reduce_scatter | solution.py:50
  482.0 206.7 %copy-start.6 = (bf16[16,128]{1,0:T(8,128)(2,1)S(1)}, bf16[16,128]{1,0:T(8,128)(2,1)}, u32[]{:S(2)}) copy-start(bf16[16,128]{1,0:T(8,128)(2,1)} %reduce-scatter.3.cloned.1.call-done) | copy-start | bytes 12292
  482.1 343.4 %copy-start.3 = (f32[128,128]{1,0:T(8,128)S(1)}, f32[128,128]{1,0:T(8,128)}, u32[]{:S(2)}) copy-start(f32[128,128]{1,0:T(8,128)} %all-reduce.11.cloned.1.call-done) | copy-start | bytes 196612
  614.2 211.3 %all-reduce.15.cloned.1.call-start = ((), (), s32[]{:S(2)}) async-start(), calls=%async_computation.7 | async-start | bytes 131072 | tf_op jit(solution)/shard_map/psum | solution.py:59
Sparse Core Ops, SparseCore 0:
  94.2 110.4 all-reduce.8
  207.3 140.9 all-reduce.10
  352.7 68.5 reduce-scatter.2
  482.1 117.6 all-reduce.12
  614.3 74.3 reduce-scatter.4
  691.2 134.2 all-reduce.14
